TPU v7x, 32 devices: a whole 2x2x4 slice. The times are simulated.
32 devices in a mesh: dp: 8 (over z, x), gate: 4 (over y, core).
Axes of the slice: x: 2, y: 2, z: 4, core: 2. Of those that a mesh axis runs over, the one named last changes fastest.
Arguments:
- inputs: bfloat16 [8, 2048, 2048], P('dp'), may hold values from -6 to 6
- weight: bfloat16 [2048, 6144], P(None, 'gate'), may hold values from -0.125 to 0.125
- ln_gain: float32 [2048], replicated, may hold values from 0.5 to 1.5
- ln_bias: float32 [2048], replicated, may hold values from -3 to 3
- forget_peep: float32 [2048], P('gate'), may hold values from -1 to 1
- reset_peep: float32 [2048], P('gate'), may hold values from -1 to 1
- forget_bias: float32 [2048], P('gate'), may hold values from 0 to 8
- reset_bias: float32 [2048], P('gate'), may hold values from -1 to 1
- resets: int32 [8, 2048], P('dp'), may hold values from 0 to 1, as said below
- padding: int32 [8, 2048], P('dp'), may hold values from 0 to 1, as said below
- grad_out: bfloat16 [8, 2048, 2048], P('dp', None, 'gate'), may hold values from -6 to 6
Outputs:
- hidden_out: bfloat16 [8, 2048, 2048], P('dp', None, 'gate')
- grad_inputs: bfloat16 [8, 2048, 2048], P('dp', None, 'gate')
- grad_weight: float32 [2048, 6144], P(None, 'gate')
- grad_ln_gain: float32 [2048], P('gate')
- grad_ln_bias: float32 [2048], P('gate')
- grad_forget_peep: float32 [2048], P('gate')
- grad_reset_peep: float32 [2048], P('gate')
- grad_forget_bias: float32 [2048], P('gate')
- grad_reset_bias: float32 [2048], P('gate')
Inputs may be any that keep to these rules, and one draw needn't show every extreme that they name: `padding`: each row holds ones followed by zeros, with more than 1536 ones; row 0 is all ones. `resets`: position 0 of every row is 1; row 0 has no other ones.
All inputs are finite; a program needn't handle non-finite values.
Results may differ from a plain program's by a relative error of at most 0.0065.
Values may be sent and summed in bfloat16 or wider, within the bound.
No kernel may reach another device: no remote copies, remote signals or barrier semaphores. Data moves between devices by JAX's collectives and lax.ppermute only.
A program may use at most 192 MiB of HBM per device.

v0:
```python
import math
import jax
import jax.numpy as jnp
from jax import lax
from jax.sharding import PartitionSpec as P

epsilon = 1e-05


def combine(earlier, later):
    early_decay, early_drive = earlier
    late_decay, late_drive = later
    return (early_decay * late_decay, late_decay * early_drive + late_drive)


def chained(decays, drives, backward):
    rows, length, channels = decays.shape
    span = math.gcd(length, 16)
    count = length // span
    dec_blocks = decays.reshape(rows, count, span, channels).transpose(2, 0, 1, 3)
    drv_blocks = drives.reshape(rows, count, span, channels).transpose(2, 0, 1, 3)
    order = list(range(span))
    if backward:
        order = order[::-1]
    run_decay = jnp.ones((rows, count, channels), jnp.float32)
    run_drive = jnp.zeros((rows, count, channels), jnp.float32)
    part_decay = [None] * span
    part_drive = [None] * span
    for step in order:
        run_decay = dec_blocks[step] * run_decay
        run_drive = dec_blocks[step] * run_drive + drv_blocks[step]
        part_decay[step] = run_decay
        part_drive[step] = run_drive
    inclusive = lax.associative_scan(combine, (run_decay, run_drive), reverse=backward, axis=1)[1]
    edge = jnp.zeros((rows, 1, channels), jnp.float32)
    if backward:
        incoming = jnp.concatenate([inclusive[:, 1:], edge], axis=1)
    else:
        incoming = jnp.concatenate([edge, inclusive[:, :-1]], axis=1)
    states = jnp.stack(
        [part_drive[step] + part_decay[step] * incoming for step in range(span)], axis=0
    )
    return states.transpose(1, 2, 0, 3).reshape(rows, length, channels)


def contract(left, right, left_dim, right_dim):
    return lax.dot_general(
        left, right, (((left_dim,), (right_dim,)), ((), ())), preferred_element_type=jnp.float32
    )


def shards(
    inputs,
    weight,
    ln_gain,
    ln_bias,
    forget_peep,
    reset_peep,
    forget_bias,
    reset_bias,
    resets,
    padding,
    grad_out,
):
    rows, length, features = inputs.shape
    tokens = rows * length
    channels = forget_peep.shape[0]
    offset = lax.axis_index("gate") * channels
    flat_rows = inputs.astype(jnp.float32).reshape(tokens, features)
    row_mean = jnp.mean(flat_rows, axis=1, keepdims=True)
    centered = flat_rows - row_mean
    inv_std = lax.rsqrt(jnp.mean(centered * centered, axis=1, keepdims=True) + epsilon)
    unit_rows = centered * inv_std
    normed = (unit_rows * ln_gain + ln_bias).astype(jnp.bfloat16)
    local_cols = jnp.dot(normed, weight, preferred_element_type=jnp.float32).astype(jnp.bfloat16)
    mixed_cols = lax.all_to_all(local_cols, "gate", split_axis=1, concat_axis=1, tiled=True)
    utilde = mixed_cols[:, :channels].astype(jnp.float32).reshape(rows, length, channels)
    uforget = (
        mixed_cols[:, channels : 2 * channels].astype(jnp.float32).reshape(rows, length, channels)
    )
    ureset = mixed_cols[:, 2 * channels :].astype(jnp.float32).reshape(rows, length, channels)
    xslice = lax.dynamic_slice_in_dim(inputs, offset, channels, 2).astype(jnp.float32)
    forget = jax.nn.sigmoid(uforget + forget_peep * xslice + forget_bias)
    reset_gate = jax.nn.sigmoid(ureset + reset_peep * xslice + reset_bias)
    carry_keep = (1 - resets).astype(jnp.float32)[:, :, None]
    decays = forget * carry_keep
    drives = (1.0 - forget) * utilde
    memory = chained(decays, drives, False)
    live_mask = padding.astype(jnp.float32)[:, :, None]
    outputs = live_mask * (reset_gate * memory + (1.0 - reset_gate) * xslice)
    grad_live = grad_out.astype(jnp.float32) * live_mask
    dreset = grad_live * (memory - xslice) * reset_gate * (1.0 - reset_gate)
    dcell_local = grad_live * reset_gate
    edge_zeros = jnp.zeros((rows, 1, channels), jnp.float32)
    decay_next = jnp.concatenate([decays[:, 1:], edge_zeros], axis=1)
    dcells = chained(decay_next, dcell_local, True)
    previous = jnp.concatenate([edge_zeros, memory[:, :-1]], axis=1)
    dtilde = dcells * (1.0 - forget)
    dforget = dcells * (previous * carry_keep - utilde) * forget * (1.0 - forget)
    direct = grad_live * (1.0 - reset_gate) + dforget * forget_peep + dreset * reset_peep
    dstreams = (
        jnp.concatenate([dtilde, dforget, dreset], axis=2)
        .reshape(tokens, 3 * channels)
        .astype(jnp.bfloat16)
    )
    dlocal = lax.all_to_all(dstreams, "gate", split_axis=1, concat_axis=1, tiled=True)
    partial_in = contract(dlocal, weight, 1, 1)
    weight_grad = contract(normed, dlocal, 0, 0)
    dnormed = lax.psum_scatter(partial_in, "gate", scatter_dimension=1, tiled=True)
    unit_slice = lax.dynamic_slice_in_dim(unit_rows, offset, channels, 1)
    gain_slice = lax.dynamic_slice_in_dim(ln_gain, offset, channels, 0)
    grad_unit = dnormed * gain_slice
    first_total, second_total = lax.psum(
        (
            jnp.sum(grad_unit, axis=1, keepdims=True),
            jnp.sum(grad_unit * unit_slice, axis=1, keepdims=True),
        ),
        "gate",
    )
    dx_norm = inv_std * (grad_unit - first_total / features - unit_slice * second_total / features)
    dinputs = (
        (dx_norm + direct.reshape(tokens, channels))
        .astype(jnp.bfloat16)
        .reshape(rows, length, channels)
    )
    totals = lax.psum(
        (
            weight_grad,
            jnp.sum(dnormed * unit_slice, axis=0),
            jnp.sum(dnormed, axis=0),
            jnp.sum(dforget * xslice, axis=(0, 1)),
            jnp.sum(dreset * xslice, axis=(0, 1)),
            jnp.sum(dforget, axis=(0, 1)),
            jnp.sum(dreset, axis=(0, 1)),
        ),
        "dp",
    )
    return (
        outputs.astype(jnp.bfloat16),
        dinputs,
        totals[0],
        totals[1],
        totals[2],
        totals[3],
        totals[4],
        totals[5],
        totals[6],
    )


def solution(mesh):
    return jax.shard_map(
        shards,
        mesh=mesh,
        in_specs=(
            P("dp", None, None),
            P(None, "gate"),
            P(),
            P(),
            P("gate"),
            P("gate"),
            P("gate"),
            P("gate"),
            P("dp", None),
            P("dp", None),
            P("dp", None, "gate"),
        ),
        out_specs=(
            P("dp", None, "gate"),
            P("dp", None, "gate"),
            P(None, "gate"),
            P("gate"),
            P("gate"),
            P("gate"),
            P("gate"),
            P("gate"),
            P("gate"),
        ),
        check_vma=False,
    )
```

profile of v0, /device:TPU:0, one launch (start us, length us, event | category | flops | bytes accessed | tf_op | source)
XLA Modules:
  0.0 1001.1 jit_solution(17736742718394757281)
XLA Ops:
  8.0 4.7 convert_reduce_fusion
  16.6 18.4 %fusion.18 = bf16[2048,1536]{0,1:T(8,128)(2,1)} fusion(bf16[2048,1536]{1,0:T(8,128)(2,1)S(1)} %copy-done.59, f32[2048]{0:T(1024)S(1)} %copy-done.60, f32[2048]{0:T(1024)S(1)} %copy-done.57, bf16[1,2048,2048]{2,1,0:T(8,128)(2,1)} %param.11, f32[2048]{0:T(1024)S(1)} %add_rsqrt_fusion, f32[2048]{0:T(1024)S(1)} %broadcast_multiply_fusion.2), kind=kOutput, calls=%fused_computation.27 | convolution fusion | flops 12913213440 | bytes 21004288 | tf_op jit(solution)/shard_map/dot_general | solution.py:75
  35.0 5.4 all-to-all-start
  40.6 71.2 %all-to-all-done = bf16[2048,4,384]{0,2,1:T(8,128)(2,1)} async-done(((bf16[2048,4,384]{0,2,1:T(8,128)(2,1)}), bf16[2048,4,384]{0,2,1:T(8,128)(2,1)}, u32[]{:S(2)}, u32[]{:S(2)}) %all-to-all-start) | async-done | bytes 6291488 | tf_op jit(solution)/shard_map/all_to_all | solution.py:76
  111.8 5.8 fusion.153
  117.6 3.1 copy.28
  120.7 3.9 copy.29
  124.6 3.9 copy.30
  128.6 7.4 convert_multiply_fusion.5
  138.5 4.3 fusion.93
  142.8 15.9 %fusion.46 = (f32[1,128,512]{2,0,1:T(1,128)S(1)}, f32[1,128,512]{2,0,1:T(1,128)}, f32[1,128,512]{2,0,1:T(1,128)}, f32[1,128,512]{2,0,1:T(1,128)}, f32[1,128,512]...) fusion(f32[16,1,128,512]{3,0,2,1:T(8,128)} %bitcast.786, ...), kind=kLoop, calls=%fused_computation.66 | loop fusion | flops 2097152 | bytes 10485760 | tf_op jit(solution)/shard_map/add | solution.py:31
  164.5 16.6 %fusion.78 = (f32[1,128,512]{2,0,1:T(1,128)S(1)}, f32[1,128,512]{2,0,1:T(1,128)}, f32[1,128,512]{2,0,1:T(1,128)}, f32[1,128,512]{2,0,1:T(1,128)}, f32[1,128,512]...) fusion(f32[16,1,128,512]{3,0,2,1:T(8,128)} %bitcast.771), kind=kLoop, calls=%fused_computation.193 | loop fusion | flops 983040 | bytes 6029312 | tf_op jit(solution)/shard_map/mul | solution.py:30
  181.1 16.4 %fusion.62 = (f32[1,128,512]{2,0,1:T(1,128)S(1)}, f32[1,128,512]{2,0,1:T(1,128)}, f32[1,128,512]{2,0,1:T(1,128)}, f32[1,128,512]{2,0,1:T(1,128)}, f32[1,128,512]...) fusion(f32[16,1,128,512]{3,0,2,1:T(8,128)} %bitcast.782, ...), kind=kLoop, calls=%fused_computation.114 | loop fusion | flops 2097152 | bytes 10485760 | tf_op jit(solution)/shard_map/add | solution.py:31
  211.4 3.2 pad.94
  220.4 4.5 pad.97
  227.8 5.6 pad.99
  234.8 5.5 pad.98
  241.6 11.0 %pad.101 = f32[1,64,512]{2,0,1:T(1,128)S(1)} pad(f32[1,32,512]{2,0,1:T(1,128)} %add.1725, f32[]{:T(128)} %constant.10.clone.1), padding=0_0_0x1_0_1x0_0_0 | pad | bytes 196612 | tf_op jit(solution)/shard_map/pad | solution.py:34
  255.0 11.0 %pad.115 = f32[1,64,512]{2,0,1:T(1,128)S(1)} pad(f32[1,32,512]{2,0,1:T(1,128)} %add.1778, f32[]{:T(128)} %constant.10.clone.1), padding=0_0_0x1_0_1x0_0_0 | pad | bytes 196612 | tf_op jit(solution)/shard_map/pad | solution.py:34
  266.7 28.5 %pad.211 = f32[1,128,512]{2,0,1:T(1,128)} pad(f32[1,64,512]{2,0,1:T(1,128)} %add.1780, f32[]{:T(128)} %constant.10.clone.1), padding=0_0_0x1_0_1x0_0_0 | pad | bytes 393220
  297.2 21.9 %pad.149 = f32[1,127,512]{2,0,1:T(1,128)S(1)} pad(f32[1,64,512]{2,0,1:T(1,128)} %pad_maximum_fusion.2, f32[]{:T(128)} %constant.10.clone.1), padding=0_0_0x0_0_1x0_0_0 | pad | bytes 391172 | tf_op jit(solution)/shard_map/slice | solution.py:37
  322.1 19.8 %pad.210 = f32[1,128,512]{2,0,1:T(1,128)} pad(f32[1,64,512]{2,0,1:T(1,128)S(1)} %add.1727, f32[]{:T(128)} %constant.10.clone.1), padding=0_0_0x1_0_1x0_0_0 | pad | bytes 393220
  342.9 19.8 %pad.147 = f32[1,127,512]{2,0,1:T(1,128)} pad(f32[1,64,512]{2,0,1:T(1,128)S(1)} %pad_maximum_fusion.1, f32[]{:T(128)} %constant.10.clone.1), padding=0_0_0x0_0_1x0_0_0 | pad | bytes 391172 | tf_op jit(solution)/shard_map/slice | solution.py:39
  364.1 7.0 add_bitcast_fusion.17
  371.2 3.3 add_bitcast_fusion.16
  374.6 3.2 add_bitcast_fusion.18
  377.8 5.1 add_bitcast_fusion.19
  383.0 3.1 add_bitcast_fusion.4
  388.6 3.2 add_bitcast_fusion
  391.8 3.2 add_bitcast_fusion.10
  395.1 4.3 add_bitcast_fusion.21
  399.4 13.4 %stack.135 = f32[16,1,128,512]{3,0,2,1:T(8,128)} concatenate(f32[1,1,128,512]{3,0,2,1:T(1,128)} %get-tuple-element.134, f32[1,1,128,512]{3,0,2,1:T(1,128)} %get-tuple-element.68, f32[1,1,128,512]{3,0,2,1:T(1,128)} %get-tuple-element.83, f32[1,1,128,512]{3,0,2,1:T(1,128)} %get-tuple-element.65, f32[1,1,128,512]{3,0,2,1:T(1,128)} %get-tuple-element.93, ...), dimensions={0} | concatenate | bytes 8388608 | tf_op jit(solution)/shard_map/stack | solution.py:40
  412.9 12.9 %stack.118 = f32[16,1,128,512]{3,0,2,1:T(8,128)} concatenate(f32[1,1,128,512]{3,0,2,1:T(1,128)} %get-tuple-element.76, f32[1,1,128,512]{3,0,2,1:T(1,128)} %get-tuple-element.82, f32[1,1,128,512]{3,0,2,1:T(1,128)} %get-tuple-element.73, f32[1,1,128,512]{3,0,2,1:T(1,128)S(1)} %copy-done.34, f32[1,1,128,512]{3,0,2,1:T(1,128)S(1)} %copy-done.32, ...), dimensions={0} | concatenate | bytes 8388608 | tf_op jit(solution)/shard_map/stack | solution.py:40
  425.8 11.7 %fusion.41 = (f32[512]{0:T(512)S(1)}, f32[512]{0:T(512)S(1)}, f32[512]{0:T(512)S(1)}, f32[512]{0:T(512)S(1)}, f32[1,2048,512]{2,1,0:T(8,128)S(1)}, /*index=5*/f3...) fusion(bf16[1,2048,2048]{2,1,0:T(8,128)(2,1)} %param.11, s32[]{:T(128)S(6)} %select_n.2, ...), kind=kLoop, calls=%fused_computation.53 | loop fusion | flops 44038144 | bytes 35682308 | tf_op jit(solution)/shard_map/reduce_sum | solution.py:132
  443.8 11.4 %convert_element_type.48 = bf16[2048,4,384]{2,1,0:T(4,128)(2,1)} reshape(bf16[1,2048,1536]{2,1,0:T(8,128)(2,1)} %pad_maximum_fusion) | data formatting | bytes 12582912 | tf_op jit(solution)/shard_map/convert_element_type | solution.py:104
  455.1 3.6 copy.25
  458.7 74.4 %all_to_all.21 = bf16[2048,4,384]{2,0,1:T(8,128)(2,1)} all-to-all(bf16[2048,4,384]{2,0,1:T(8,128)(2,1)S(1)} %copy.25), channel_id=1, replica_groups=mesh['dp'=8,'gate'=4] {'gate'}, dimensions={1} | all-to-all | bytes 12582912 | tf_op jit(solution)/shard_map/all_to_all | solution.py:106
  533.2 8.7 copy.26
  541.8 20.5 %fusion.160 = f32[2048,2048]{1,0:T(8,128)} fusion(bf16[2048,1536]{0,1:T(8,128)(2,1)} %bitcast.791, bf16[2048,1536]{1,0:T(8,128)(2,1)} %param.12), kind=kOutput, calls=%fused_computation.308 | convolution fusion | flops 12884901888 | bytes 29360128 | tf_op jit(solution)/shard_map/dot_general | solution.py:47
  563.1 23.3 %fusion.10 = f32[2048,1536]{1,0:T(8,128)} fusion(bf16[2048,1536]{0,1:T(8,128)(2,1)} %bitcast.792, bf16[1,2048,2048]{2,1,0:T(8,128)(2,1)} %param.11, f32[2048]{0:T(1024)S(1)} %copy-done.61, f32[2048]{0:T(1024)S(1)} %copy-done.58, f32[2048]{0:T(1024)S(1)} %copy-done.41, f32[2048]{0:T(1024)S(1)} %copy-done.43), kind=kOutput, calls=%fused_computation.20 | convolution fusion | flops 12910067712 | bytes 27295744 | tf_op jit(solution)/shard_map/dot_general | solution.py:47
  586.5 12.6 %fusion.1 = f32[2048,2048]{1,0:T(8,128)} fusion(bf16[1,2048,2048]{2,1,0:T(8,128)(2,1)} %param.11, f32[2048]{0:T(1024)S(1)} %copy-done.41, f32[2048]{0:T(1024)S(1)} %copy-done.43), kind=kLoop, calls=%fused_computation.4 | loop fusion | flops 12582912 | bytes 25182208 | tf_op jit(solution)/shard_map/mul | solution.py:73
  599.1 89.5 %reduce-scatter.2.cloned.1.call-done = f32[2048,512]{1,0:T(8,128)} async-done(((f32[2048,2048]{1,0:T(8,128)}), f32[2048,512]{1,0:T(8,128)}) %reduce-scatter.2.cloned.1.call-update) | async-done | bytes 4194320 | tf_op jit(solution)/shard_map/reduce_scatter | solution.py:109
  688.6 5.1 multiply_reduce_fusion
  693.7 39.1 %all-reduce.32 = (f32[512]{0:T(512)}, f32[512]{0:T(512)}, f32[512]{0:T(512)}, f32[512]{0:T(512)}, f32[512]{0:T(512)}, /*index=5*/f32[512]{0:T(512)}) all-reduce(f32[512]{0:T(512)S(1)} %get-tuple-element.9, f32[512]{0:T(512)S(1)} %get-tuple-element.16, f32[512]{0:T(512)S(1)} %get-tuple-element.12, ...), channel_id=1, replica_groups=mesh['dp'=8,'gate'=4] {'dp'}, use_global_device_ids=true, to_apply=%region_9.0 | all-reduce | flops 3072 | bytes 24576 | tf_op jit(solution)/shard_map/psum | solution.py:126
  732.8 10.6 %all-reduce.33 = (f32[2048]{0:T(1024)S(1)}, f32[2048,1]{0,1:T(1,128)S(1)}) all-reduce(f32[2048]{0:T(1024)S(1)} %get-tuple-element.10, f32[2048,1]{0,1:T(1,128)S(1)} %bitcast.799), channel_id=1, replica_groups=mesh['dp'=8,'gate'=4] {'gate'}, use_global_device_ids=true, to_apply=%region_6.0 | all-reduce | flops 4096 | bytes 32768 | tf_op jit(solution)/shard_map/psum | solution.py:113
  743.3 10.2 %fusion.45 = bf16[1,2048,512]{2,1,0:T(8,128)(2,1)} fusion(f32[1,2048,512]{2,1,0:T(8,128)} %copy-done.7, f32[512]{0:T(512)S(1)} %copy-done.51, f32[1,2048,512]{2,1,0:T(8,128)} %copy-done.6, f32[512]{0:T(512)S(1)} %copy-done.47, f32[2048]{0:T(1024)S(1)} %bitcast.795, bf16[1,2048,512]{2,1,0:T(8,128)(2,1)} %param.21, f32[2048]{0:T(1024)S(1)} %get-tuple-element.23, ...), kind=kLoop, calls=%fused_computation.64 | loop fusion | flops 25165824 | bytes 25206788 | tf_op jit(solution)/shard_map/reshape | solution.py:124
  753.5 229.0 %all-reduce.36.cloned.1.call-done = f32[2048,1536]{1,0:T(8,128)} async-done(((f32[2048,1536]{1,0:T(8,128)}), f32[2048,1536]{1,0:T(8,128)}) %all-reduce.36.cloned.1.call-update) | async-done | bytes 12582928 | tf_op jit(solution)/shard_map/psum | solution.py:126
  982.6 10.6 %copy.32 = f32[2048,1536]{1,0:T(8,128)} copy(f32[2048,1536]{1,0:T(8,128)} %all-reduce.36.cloned.1.call-done) | data formatting | bytes 25165824
  (222 shorter events, 57.4 us)
Async XLA Ops:
  8.0 5.8 copy-start
  16.6 18.4 %copy-start.40 = (f32[2048]{0:T(1024)}, f32[2048]{0:T(1024)S(1)}, u32[]{:S(2)}) copy-start(f32[2048]{0:T(1024)S(1)} %add_rsqrt_fusion) | copy-start | bytes 24580
  35.0 76.8 %all-to-all-start = ((bf16[2048,4,384]{0,2,1:T(8,128)(2,1)}), bf16[2048,4,384]{0,2,1:T(8,128)(2,1)}, u32[]{:S(2)}, u32[]{:S(2)}) async-start(bf16[2048,4,384]{0,2,1:T(8,128)(2,1)} %bitcast.790), calls=%async_computation | async-start | bytes 12582912 | tf_op jit(solution)/shard_map/all_to_all | solution.py:76
  40.4 648.1 %reduce-scatter.2.cloned.1.call-start = ((), (), s32[]{:S(2)}) async-start(), calls=%async_computation.3 | async-start | bytes 20971520 | tf_op jit(solution)/shard_map/reduce_scatter | solution.py:109
  40.5 88.0 %copy-start.37 = (f32[1,2048]{1,0:T(1,128)}, f32[1,2048]{1,0:T(1,128)S(1)}, u32[]{:S(2)}) copy-start(f32[1,2048]{1,0:T(1,128)S(1)} %convert_element_type.40) | copy-start | bytes 24580
  40.6 88.0 %copy-start.44 = (f32[1,2048]{1,0:T(1,128)}, f32[1,2048]{1,0:T(1,128)S(1)}, u32[]{:S(2)}) copy-start(f32[1,2048]{1,0:T(1,128)S(1)} %subtract_convert_fusion) | copy-start | bytes 24580
  120.7 7.9 copy-start.46
  120.7 7.9 copy-start.48
  120.7 7.9 copy-start.50
  120.7 7.9 copy-start.55
  138.5 20.2 %copy-start.4 = (f32[1,2048,512]{2,1,0:T(8,128)}, f32[1,2048,512]{2,1,0:T(8,128)S(1)}, u32[]{:S(2)}) copy-start(f32[1,2048,512]{2,1,0:T(8,128)S(1)} %concatenate.59) | copy-start | bytes 12582916
  161.2 19.9 %copy-start.2 = (f32[1,2048,512]{2,1,0:T(8,128)S(1)}, f32[1,2048,512]{2,1,0:T(8,128)}, u32[]{:S(2)}) copy-start(f32[1,2048,512]{2,1,0:T(8,128)} %copy-done.1) | copy-start | bytes 12582916
  220.4 76.0 %copy-start.52 = (f32[1,1,512]{2,0,1:T(1,128)S(1)}, f32[1,1,512]{2,0,1:T(1,128)}, u32[]{:S(2)}) copy-start(f32[1,1,512]{2,0,1:T(1,128)} %slice.857) | copy-start | bytes 6148
  362.6 8.6 copy-start.19
  362.7 8.6 copy-start.20
  362.7 8.6 copy-start.21
  362.7 8.6 copy-start.22
  362.7 8.6 copy-start.23
  364.1 18.8 %copy-start.8 = (f32[1,2048,512]{2,1,0:T(8,128)S(1)}, f32[1,2048,512]{2,1,0:T(8,128)}, u32[]{:S(2)}) copy-start(f32[1,2048,512]{2,1,0:T(8,128)} %get-tuple-element.77) | copy-start | bytes 12582916
  371.2 6.6 copy-start.3
  371.2 6.6 copy-start.18
  374.5 8.4 copy-start.5
  374.5 8.4 copy-start.12
  374.5 8.4 copy-start.13
  374.5 8.4 copy-start.14
  374.5 8.4 copy-start.15
  374.6 8.4 copy-start.16
  374.6 8.4 copy-start.17
  377.8 8.4 copy-start.9
  377.8 8.4 copy-start.10
  382.9 5.7 copy-start.11
  382.9 5.7 copy-start.26
  382.9 5.7 copy-start.27
  386.2 5.7 copy-start.24
  388.6 6.5 copy-start.28
  388.6 6.5 copy-start.29
  399.4 13.4 %copy-start.30 = (f32[1,1,128,512]{3,0,2,1:T(1,128)S(1)}, f32[1,1,128,512]{3,0,2,1:T(1,128)}, u32[]{:S(2)}) copy-start(f32[1,1,128,512]{3,0,2,1:T(1,128)} %get-tuple-element.69) | copy-start | bytes 786436
  399.4 13.4 %copy-start.31 = (f32[1,1,128,512]{3,0,2,1:T(1,128)S(1)}, f32[1,1,128,512]{3,0,2,1:T(1,128)}, u32[]{:S(2)}) copy-start(f32[1,1,128,512]{3,0,2,1:T(1,128)} %get-tuple-element.70) | copy-start | bytes 786436
  399.4 13.4 %copy-start.32 = (f32[1,1,128,512]{3,0,2,1:T(1,128)S(1)}, f32[1,1,128,512]{3,0,2,1:T(1,128)}, u32[]{:S(2)}) copy-start(f32[1,1,128,512]{3,0,2,1:T(1,128)} %get-tuple-element.71) | copy-start | bytes 786436
  399.4 13.4 %copy-start.33 = (f32[1,1,128,512]{3,0,2,1:T(1,128)S(1)}, f32[1,1,128,512]{3,0,2,1:T(1,128)}, u32[]{:S(2)}) copy-start(f32[1,1,128,512]{3,0,2,1:T(1,128)} %get-tuple-element.96) | copy-start | bytes 786436
  399.4 13.4 %copy-start.34 = (f32[1,1,128,512]{3,0,2,1:T(1,128)S(1)}, f32[1,1,128,512]{3,0,2,1:T(1,128)}, u32[]{:S(2)}) copy-start(f32[1,1,128,512]{3,0,2,1:T(1,128)} %get-tuple-element.97) | copy-start | bytes 786436
  412.9 12.9 %copy-start.38 = (f32[1,2048]{1,0:T(1,128)S(1)}, f32[1,2048]{1,0:T(1,128)}, u32[]{:S(2)}) copy-start(f32[1,2048]{1,0:T(1,128)} %copy-done.37) | copy-start | bytes 24580
  412.9 12.9 %copy-start.45 = (f32[1,2048]{1,0:T(1,128)S(1)}, f32[1,2048]{1,0:T(1,128)}, u32[]{:S(2)}) copy-start(f32[1,2048]{1,0:T(1,128)} %copy-done.44) | copy-start | bytes 24580
  412.9 12.9 %copy-start.47 = (f32[512]{0:T(512)S(1)}, f32[512]{0:T(512)}, u32[]{:S(2)}) copy-start(f32[512]{0:T(512)} %param.15) | copy-start | bytes 6148
  412.9 12.9 %copy-start.49 = (f32[512]{0:T(512)S(1)}, f32[512]{0:T(512)}, u32[]{:S(2)}) copy-start(f32[512]{0:T(512)} %param.18) | copy-start | bytes 6148
  412.9 12.9 %copy-start.51 = (f32[512]{0:T(512)S(1)}, f32[512]{0:T(512)}, u32[]{:S(2)}) copy-start(f32[512]{0:T(512)} %param.16) | copy-start | bytes 6148
  412.9 12.9 %copy-start.56 = (f32[512]{0:T(512)S(1)}, f32[512]{0:T(512)}, u32[]{:S(2)}) copy-start(f32[512]{0:T(512)} %param.17) | copy-start | bytes 6148
  562.4 420.1 %all-reduce.36.cloned.1.call-start = ((), (), s32[]{:S(2)}) async-start(), calls=%async_computation.4 | async-start | bytes 25165824 | tf_op jit(solution)/shard_map/psum | solution.py:126
  (17 other events, 39.1 us)
Sparse Core Ops, SparseCore 0:
  562.6 125.9 reduce-scatter.1
Sparse Core Ops, SparseCore 1:
  586.5 396.0 all-reduce.35
where the time goes:
time: 1020 us; the launch traced here: 1000 us
  waiting for transfers between devices  390 us (38%)
  local copies, waits for them, and re-layouts  232 us (23%)
  other arithmetic  170 us (17%)
  blocking collectives  124 us (12%)
  matrix products  62.2 us (6%)
  between operations  17 us (2%)
    psum x1, waiting for transfers between devices, shards(): lax.psum((weight_grad, jnp.sum(dnormed * unit_slice, axis=0), jnp.sum(dno...  229 us
    reduce_scatter x1, waiting for transfers between devices, shards(): lax.psum_scatter(partial_in, 'gate', scatter_dimension=1, tiled=True)  89.5 us
    unnamed x130, local copies, waits for them, and re-layouts  77.5 us
    all_to_all x1, blocking collectives, shards(): lax.all_to_all(dstreams, 'gate', split_axis=1, concat_axis=1, tiled=True)  74.4 us
    all_to_all x1, waiting for transfers between devices, shards(): lax.all_to_all(local_cols, 'gate', split_axis=1, concat_axis=1, tiled=True)  71.2 us
    pad x20, local copies, waits for them, and re-layouts, chained(): lax.associative_scan(combine, (run_decay, run_drive), reverse=backward, a...  50.7 us
    dot_general x2, matrix products, contract(): lax.dot_general(left, right, (((left_dim,), (right_dim,)), ((), ())), pre...  43.8 us
    psum x1, blocking collectives, shards(): lax.psum((weight_grad, jnp.sum(dnormed * unit_slice, axis=0), jnp.sum(dno...  39.1 us
  transfers between devices with their start and end apart: 3, of which 3 were waited for; matrix products, arithmetic and copies ran while one was open for 5% of the time, Pallas kernels for 0%

commit v1 on v0

--- a/solution.py
+++ b/solution.py
@@ -1,3 +1,4 @@
+import functools
 import math
 import jax
 import jax.numpy as jnp
@@ -5,6 +6,31 @@
 from jax.sharding import PartitionSpec as P
 
 epsilon = 1e-05
+
+
+def cover_weights(frame, k_dim, dim_no):
+    field_out = lax.axis_index("gate")
+    last = lax.axis_size("gate")
+    prior, item_now = (last, field_out)
+    v_now = list(frame.shape)
+    taken_in = frame.shape[k_dim] // prior
+    v_now[k_dim] = taken_in
+    extra = v_now[dim_no]
+    v_now[dim_no] = extra * prior
+    local_next = jnp.zeros(v_now, frame.dtype)
+    for dev in tuple(range(prior)):
+        x_new = lax.dynamic_slice_in_dim(frame, (item_now ^ dev) * taken_in, taken_in, axis=k_dim)
+        if dev:
+            x_new = lax.ppermute(
+                x_new, axis_name="gate", perm=[(src_i, src_i ^ dev) for src_i in range(prior)]
+            )
+        local_next = lax.dynamic_update_slice_in_dim(
+            local_next, x_new, (item_now ^ dev) * extra, axis=dim_no
+        )
+    return local_next
+
+
+_perform_forms = functools.partial(cover_weights, k_dim=1, dim_no=1)
 
 
 def combine(earlier, later):
@@ -73,7 +99,7 @@
     unit_rows = centered * inv_std
     normed = (unit_rows * ln_gain + ln_bias).astype(jnp.bfloat16)
     local_cols = jnp.dot(normed, weight, preferred_element_type=jnp.float32).astype(jnp.bfloat16)
-    mixed_cols = lax.all_to_all(local_cols, "gate", split_axis=1, concat_axis=1, tiled=True)
+    mixed_cols = _perform_forms(local_cols)
     utilde = mixed_cols[:, :channels].astype(jnp.float32).reshape(rows, length, channels)
     uforget = (
         mixed_cols[:, channels : 2 * channels].astype(jnp.float32).reshape(rows, length, channels)

time: 1020 us -> 888 us (0.87); the launches traced: 1000 us -> 882 us
  local copies, waits for them, and re-layouts: 232 us -> 146 us
  other arithmetic: 170 us -> 148 us
    all_to_all x1 -> x0, waiting for transfers between devices: 71.2 us -> none  [shards(): lax.all_to_all(local_cols, 'gate', split_axis=1, concat_axis=1, tiled=True)]
    ppermute x0 -> x3, waiting for transfers between devices: none -> 64.2 us  [cover_weights(): lax.ppermute(x_new, axis_name='gate', perm=[(src_i, src_i ^ dev) for src_...]
    pad x20, local copies, waits for them, and re-layouts: 50.7 us -> 3.52 us  [chained(): lax.associative_scan(combine, (run_decay, run_drive), reverse=backward, a...]
    unnamed x130 -> x129, local copies, waits for them, and re-layouts: 77.5 us -> 56 us
    slice x2, local copies, waits for them, and re-layouts: 22.9 us -> 1.89 us  [chained(): incoming = jnp.concatenate([inclusive[:, 1:], edge], axis=1)]
  transfers between devices with their start and end apart: 3 -> 5, of which waited for: 3 -> 5; matrix products, arithmetic and copies ran while one was open for 5% -> 6% of each run, Pallas kernels for 0% -> 0%
where the time goes in v1:
time: 888 us; the launch traced here: 882 us
  waiting for transfers between devices  383 us (43%)
  other arithmetic  148 us (17%)
  local copies, waits for them, and re-layouts  146 us (16%)
  blocking collectives  124 us (14%)
  matrix products  61.8 us (7%)
  between operations  16.8 us (2%)
    psum x1, waiting for transfers between devices, shards(): lax.psum((weight_grad, jnp.sum(dnormed * unit_slice, axis=0), jnp.sum(dno...  229 us
    reduce_scatter x1, waiting for transfers between devices, shards(): lax.psum_scatter(partial_in, 'gate', scatter_dimension=1, tiled=True)  89.1 us
    all_to_all x1, blocking collectives, shards(): lax.all_to_all(dstreams, 'gate', split_axis=1, concat_axis=1, tiled=True)  74.2 us
    ppermute x3, waiting for transfers between devices, cover_weights(): lax.ppermute(x_new, axis_name='gate', perm=[(src_i, src_i ^ dev) for src_...  64.2 us
    unnamed x129, local copies, waits for them, and re-layouts  56 us
    dot_general x2, matrix products, contract(): lax.dot_general(left, right, (((left_dim,), (right_dim,)), ((), ())), pre...  43.6 us
    psum x1, blocking collectives, shards(): lax.psum((weight_grad, jnp.sum(dnormed * unit_slice, axis=0), jnp.sum(dno...  39.2 us
    another operation x9, other arithmetic, chained(): jnp.stack([part_drive[step] + part_decay[step] * incoming for step in ran...  33.3 us
  transfers between devices with their start and end apart: 5, of which 5 were waited for; matrix products, arithmetic and copies ran while one was open for 6% of the time, Pallas kernels for 0%

profile of v1, /device:TPU:0, one launch (start us, length us, event | category | flops | bytes accessed | tf_op | source)
XLA Modules:
  0.0 881.9 jit_solution(8359658109291107222)
XLA Ops:
  8.1 4.7 convert_reduce_fusion
  13.8 2.3 fusion.3
  16.2 18.2 %fusion.18 = bf16[2048,1536]{1,0:T(8,128)(2,1)S(1)} fusion(bf16[2048,1536]{1,0:T(8,128)(2,1)} %param.12, f32[2048]{0:T(1024)S(1)} %copy-done.61, f32[2048]{0:T(1024)S(1)} %copy-done.59, bf16[1,2048,2048]{2,1,0:T(8,128)(2,1)} %param.11, f32[2048]{0:T(1024)S(1)} %add_rsqrt_fusion, f32[2048]{0:T(1024)S(1)} %broadcast_multiply_fusion.2), kind=kOutput, calls=%fused_computation.27 | convolution fusion | flops 12913213440 | bytes 21004288 | tf_op jit(solution)/shard_map/dot_general | solution.py:101
  34.5 3.0 broadcast_in_dim.6
  37.5 2.9 constant_dynamic-slice_fusion
  40.9 2.6 collective-permute-start.1
  44.3 2.9 constant_dynamic-update-slice_fusion.2
  47.2 31.7 %collective-permute-done.1 = bf16[2048,384]{1,0:T(8,128)(2,1)S(1)} collective-permute-done((bf16[2048,384]{1,0:T(8,128)(2,1)}, bf16[2048,384]{1,0:T(8,128)(2,1)S(1)}, u32[]{:S(2)}, u32[]{:S(2)}) %collective-permute-start.1) | collective-permute-done | bytes 1572896 | tf_op jit(solution)/shard_map/ppermute | solution.py:24
  78.9 1.5 constant_dynamic-update-slice_fusion.1
  80.4 31.9 %collective-permute-done.2 = bf16[2048,384]{1,0:T(8,128)(2,1)S(1)} collective-permute-done((bf16[2048,384]{1,0:T(8,128)(2,1)}, bf16[2048,384]{1,0:T(8,128)(2,1)S(1)}, u32[]{:S(2)}, u32[]{:S(2)}) %collective-permute-start.2) | collective-permute-done | bytes 1572896 | tf_op jit(solution)/shard_map/ppermute | solution.py:24
  113.7 7.8 convert_multiply_fusion.5
  122.0 1.5 copy-done.1
  124.0 4.4 fusion.93
  128.4 7.3 fusion.46
  141.0 16.8 %fusion.78 = (f32[1,128,512]{2,0,1:T(1,128)S(1)}, f32[1,128,512]{2,0,1:T(1,128)}, f32[1,128,512]{2,0,1:T(1,128)}, f32[1,128,512]{2,0,1:T(1,128)}, f32[1,128,512]...) fusion(f32[16,1,128,512]{3,0,2,1:T(8,128)} %bitcast.776), kind=kLoop, calls=%fused_computation.197 | loop fusion | flops 983040 | bytes 6029312 | tf_op jit(solution)/shard_map/mul | solution.py:56
  157.9 15.9 %fusion.62 = (f32[1,128,512]{2,0,1:T(1,128)S(1)}, f32[1,128,512]{2,0,1:T(1,128)}, f32[1,128,512]{2,0,1:T(1,128)}, f32[1,128,512]{2,0,1:T(1,128)}, f32[1,128,512]...) fusion(f32[16,1,128,512]{3,0,2,1:T(8,128)} %bitcast.787, ...), kind=kLoop, calls=%fused_computation.118 | loop fusion | flops 2097152 | bytes 10485760 | tf_op jit(solution)/shard_map/add | solution.py:57
  179.7 19.6 %pad.211 = f32[1,128,512]{2,0,1:T(1,128)} pad(f32[1,64,512]{2,0,1:T(1,128)S(1)} %add.1800, f32[]{:T(128)} %constant.16.clone.1), padding=0_0_0x1_0_1x0_0_0 | pad | bytes 393220
  202.2 1.9 slice_add_fusion.15
  205.1 19.6 %pad.210 = f32[1,128,512]{2,0,1:T(1,128)} pad(f32[1,64,512]{2,0,1:T(1,128)S(1)} %add.1747, f32[]{:T(128)} %constant.16.clone.1), padding=0_0_0x1_0_1x0_0_0 | pad | bytes 393220
  225.7 19.5 %pad.147 = f32[1,127,512]{2,0,1:T(1,128)} pad(f32[1,64,512]{2,0,1:T(1,128)S(1)} %pad_maximum_fusion.1, f32[]{:T(128)} %constant.16.clone.1), padding=0_0_0x0_0_1x0_0_0 | pad | bytes 391172 | tf_op jit(solution)/shard_map/slice | solution.py:65
  245.2 1.4 slice_add_fusion.16
  246.6 7.0 add_bitcast_fusion.17
  253.7 3.4 add_bitcast_fusion.16
  257.1 1.9 add_bitcast_fusion.18
  259.0 5.1 add_bitcast_fusion.19
  264.2 3.0 add_bitcast_fusion.4
  267.2 2.2 add_bitcast_fusion.3
  269.4 3.2 add_bitcast_fusion
  272.7 3.2 add_bitcast_fusion.10
  275.9 4.3 add_bitcast_fusion.21
  280.3 12.9 %stack.135 = f32[16,1,128,512]{3,0,2,1:T(8,128)} concatenate(f32[1,1,128,512]{3,0,2,1:T(1,128)} %get-tuple-element.135, f32[1,1,128,512]{3,0,2,1:T(1,128)} %get-tuple-element.69, f32[1,1,128,512]{3,0,2,1:T(1,128)} %get-tuple-element.84, f32[1,1,128,512]{3,0,2,1:T(1,128)S(1)} %copy-done.37, f32[1,1,128,512]{3,0,2,1:T(1,128)S(1)} %copy-done.40, ...), dimensions={0} | concatenate | bytes 8388608 | tf_op jit(solution)/shard_map/stack | solution.py:66
  293.4 13.0 %stack.118 = f32[16,1,128,512]{3,0,2,1:T(8,128)} concatenate(f32[1,1,128,512]{3,0,2,1:T(1,128)} %get-tuple-element.77, f32[1,1,128,512]{3,0,2,1:T(1,128)} %get-tuple-element.83, f32[1,1,128,512]{3,0,2,1:T(1,128)} %get-tuple-element.74, f32[1,1,128,512]{3,0,2,1:T(1,128)S(1)} %copy-done.35, f32[1,1,128,512]{3,0,2,1:T(1,128)S(1)} %copy-done.33, ...), dimensions={0} | concatenate | bytes 8388608 | tf_op jit(solution)/shard_map/stack | solution.py:66
  306.4 13.0 %fusion.41 = (f32[512]{0:T(512)S(1)}, f32[512]{0:T(512)S(1)}, f32[512]{0:T(512)S(1)}, f32[512]{0:T(512)S(1)}, f32[1,2048,512]{2,1,0:T(8,128)S(1)}, /*index=5*/f3...) fusion(bf16[1,2048,2048]{2,1,0:T(8,128)(2,1)} %param.11, s32[]{:T(128)S(6)} %select_n.25, ...), kind=kLoop, calls=%fused_computation.53 | loop fusion | flops 44038144 | bytes 35682308 | tf_op jit(solution)/shard_map/reduce_sum | solution.py:158
  322.8 2.9 pad_maximum_fusion
  325.8 11.4 %convert_element_type.48 = bf16[2048,4,384]{2,1,0:T(4,128)(2,1)} reshape(bf16[1,2048,1536]{2,1,0:T(8,128)(2,1)} %pad_maximum_fusion) | data formatting | bytes 12582912 | tf_op jit(solution)/shard_map/convert_element_type | solution.py:130
  337.2 3.6 copy.21
  340.8 74.2 %all_to_all.9 = bf16[2048,4,384]{2,0,1:T(8,128)(2,1)} all-to-all(bf16[2048,4,384]{2,0,1:T(8,128)(2,1)S(1)} %copy.21), channel_id=1, replica_groups=mesh['dp'=8,'gate'=4] {'gate'}, dimensions={1} | all-to-all | bytes 12582912 | tf_op jit(solution)/shard_map/all_to_all | solution.py:132
  415.0 8.7 copy.22
  423.7 20.6 %fusion.159 = f32[2048,2048]{1,0:T(8,128)} fusion(bf16[2048,1536]{0,1:T(8,128)(2,1)} %bitcast.795, bf16[2048,1536]{1,0:T(8,128)(2,1)} %param.12), kind=kOutput, calls=%fused_computation.317 | convolution fusion | flops 12884901888 | bytes 29360128 | tf_op jit(solution)/shard_map/dot_general | solution.py:73
  445.0 23.0 %fusion.10 = f32[2048,1536]{1,0:T(8,128)} fusion(bf16[2048,1536]{0,1:T(8,128)(2,1)} %bitcast.796, bf16[1,2048,2048]{2,1,0:T(8,128)(2,1)} %param.11, f32[2048]{0:T(1024)S(1)} %copy-done.62, f32[2048]{0:T(1024)S(1)} %copy-done.60, f32[2048]{0:T(1024)S(1)} %copy-done.45, f32[2048]{0:T(1024)S(1)} %copy-done.47), kind=kOutput, calls=%fused_computation.20 | convolution fusion | flops 12910067712 | bytes 27295744 | tf_op jit(solution)/shard_map/dot_general | solution.py:73
  468.1 12.3 %fusion.1 = f32[2048,2048]{1,0:T(8,128)} fusion(bf16[1,2048,2048]{2,1,0:T(8,128)(2,1)} %param.11, f32[2048]{0:T(1024)S(1)} %copy-done.45, f32[2048]{0:T(1024)S(1)} %copy-done.47), kind=kLoop, calls=%fused_computation.4 | loop fusion | flops 12582912 | bytes 25182208 | tf_op jit(solution)/shard_map/mul | solution.py:99
  480.4 89.1 %reduce-scatter.2.cloned.1.call-done = f32[2048,512]{1,0:T(8,128)} async-done(((f32[2048,2048]{1,0:T(8,128)}), f32[2048,512]{1,0:T(8,128)}) %reduce-scatter.2.cloned.1.call-update) | async-done | bytes 4194320 | tf_op jit(solution)/shard_map/reduce_scatter | solution.py:135
  569.5 5.1 multiply_reduce_fusion
  574.6 39.2 %all-reduce.32 = (f32[512]{0:T(512)}, f32[512]{0:T(512)}, f32[512]{0:T(512)}, f32[512]{0:T(512)}, f32[512]{0:T(512)}, /*index=5*/f32[512]{0:T(512)}) all-reduce(f32[512]{0:T(512)S(1)} %get-tuple-element.9, f32[512]{0:T(512)S(1)} %get-tuple-element.16, f32[512]{0:T(512)S(1)} %get-tuple-element.12, ...), channel_id=1, replica_groups=mesh['dp'=8,'gate'=4] {'dp'}, use_global_device_ids=true, to_apply=%region_9.0 | all-reduce | flops 3072 | bytes 24576 | tf_op jit(solution)/shard_map/psum | solution.py:152
  613.8 10.4 %all-reduce.33 = (f32[2048]{0:T(1024)S(1)}, f32[2048,1]{0,1:T(1,128)S(1)}) all-reduce(f32[2048]{0:T(1024)S(1)} %get-tuple-element.10, f32[2048,1]{0,1:T(1,128)S(1)} %bitcast.803), channel_id=1, replica_groups=mesh['dp'=8,'gate'=4] {'gate'}, use_global_device_ids=true, to_apply=%region_6.0 | all-reduce | flops 4096 | bytes 32768 | tf_op jit(solution)/shard_map/psum | solution.py:139
  624.2 10.1 %fusion.45 = bf16[1,2048,512]{2,1,0:T(8,128)(2,1)} fusion(f32[1,2048,512]{2,1,0:T(8,128)} %copy-done.7, f32[512]{0:T(512)S(1)} %copy-done.54, f32[1,2048,512]{2,1,0:T(8,128)} %copy-done.6, f32[512]{0:T(512)S(1)} %copy-done.50, f32[2048]{0:T(1024)S(1)} %bitcast.799, bf16[1,2048,512]{2,1,0:T(8,128)(2,1)S(1)} %copy-done.11, f32[2048]{0:T(1024)S(1)} %get-tuple-element.23, ...), kind=kLoop, calls=%fused_computation.67 | loop fusion | flops 25165824 | bytes 25206788 | tf_op jit(solution)/shard_map/reshape | solution.py:150
  634.3 229.3 %all-reduce.36.cloned.1.call-done = f32[2048,1536]{1,0:T(8,128)} async-done(((f32[2048,1536]{1,0:T(8,128)}), f32[2048,1536]{1,0:T(8,128)}) %all-reduce.36.cloned.1.call-update) | async-done | bytes 12582928 | tf_op jit(solution)/shard_map/psum | solution.py:152
  863.6 10.6 %copy.28 = f32[2048,1536]{1,0:T(8,128)} copy(f32[2048,1536]{1,0:T(8,128)} %all-reduce.36.cloned.1.call-done) | data formatting | bytes 25165824
  (229 shorter events, 24.9 us)
Async XLA Ops:
  8.0 561.5 %reduce-scatter.2.cloned.1.call-start = ((), (), s32[]{:S(2)}) async-start(), calls=%async_computation.2 | async-start | bytes 20971520 | tf_op jit(solution)/shard_map/reduce_scatter | solution.py:135
  16.2 18.3 %copy-start.44 = (f32[2048]{0:T(1024)}, f32[2048]{0:T(1024)S(1)}, u32[]{:S(2)}) copy-start(f32[2048]{0:T(1024)S(1)} %add_rsqrt_fusion) | copy-start | bytes 24580
  40.4 3.9 collective-permute-start
  40.9 38.0 %collective-permute-start.1 = (bf16[2048,384]{1,0:T(8,128)(2,1)}, bf16[2048,384]{1,0:T(8,128)(2,1)S(1)}, u32[]{:S(2)}, u32[]{:S(2)}) collective-permute-start(bf16[2048,384]{1,0:T(8,128)(2,1)} %get-tuple-element.79), channel_id=1, source_target_pairs={{0,2},{1,3},{2,0},{3,1},{4,6},{5,7},{6,4},{7,5},{8,10},{9,11},{10,... | collective-permute-start | bytes 4718600 | tf_op jit(solution)/shard_map/ppermute | solution.py:24
  43.5 68.8 %collective-permute-start.2 = (bf16[2048,384]{1,0:T(8,128)(2,1)}, bf16[2048,384]{1,0:T(8,128)(2,1)S(1)}, u32[]{:S(2)}, u32[]{:S(2)}) collective-permute-start(bf16[2048,384]{1,0:T(8,128)(2,1)} %get-tuple-element.78), channel_id=1, source_target_pairs={{0,3},{1,2},{2,1},{3,0},{4,7},{5,6},{6,5},{7,4},{8,11},{9,10},{10,... | collective-permute-start | bytes 4718600 | tf_op jit(solution)/shard_map/ppermute | solution.py:24
  43.6 70.0 %copy-start.42 = (f32[1,2048]{1,0:T(1,128)}, f32[1,2048]{1,0:T(1,128)S(1)}, u32[]{:S(2)}) copy-start(f32[1,2048]{1,0:T(1,128)S(1)} %convert_element_type.40) | copy-start | bytes 24580
  43.6 70.0 %copy-start.48 = (f32[1,2048]{1,0:T(1,128)}, f32[1,2048]{1,0:T(1,128)S(1)}, u32[]{:S(2)}) copy-start(f32[1,2048]{1,0:T(1,128)S(1)} %subtract_convert_fusion) | copy-start | bytes 24580
  44.3 69.4 %copy-start.10 = (bf16[1,2048,512]{2,1,0:T(8,128)(2,1)S(1)}, bf16[1,2048,512]{2,1,0:T(8,128)(2,1)}, u32[]{:S(2)}) copy-start(bf16[1,2048,512]{2,1,0:T(8,128)(2,1)} %param.21) | copy-start | bytes 6291460
  44.3 69.4 %copy-start.50 = (f32[512]{0:T(512)S(1)}, f32[512]{0:T(512)}, u32[]{:S(2)}) copy-start(f32[512]{0:T(512)} %param.15) | copy-start | bytes 6148
  44.3 69.4 %copy-start.51 = (f32[512]{0:T(512)S(1)}, f32[512]{0:T(512)}, u32[]{:S(2)}) copy-start(f32[512]{0:T(512)} %param.18) | copy-start | bytes 6148
  44.3 69.4 %copy-start.53 = (f32[512]{0:T(512)S(1)}, f32[512]{0:T(512)}, u32[]{:S(2)}) copy-start(f32[512]{0:T(512)} %param.16) | copy-start | bytes 6148
  44.3 69.4 %copy-start.57 = (f32[512]{0:T(512)S(1)}, f32[512]{0:T(512)}, u32[]{:S(2)}) copy-start(f32[512]{0:T(512)} %param.17) | copy-start | bytes 6148
  121.5 6.9 copy-start.8
  124.0 11.7 %copy-start.4 = (f32[1,2048,512]{2,1,0:T(8,128)}, f32[1,2048,512]{2,1,0:T(8,128)S(1)}, u32[]{:S(2)}) copy-start(f32[1,2048,512]{2,1,0:T(8,128)S(1)} %concatenate.59) | copy-start | bytes 12582916
  138.3 19.6 %copy-start.2 = (f32[1,2048,512]{2,1,0:T(8,128)S(1)}, f32[1,2048,512]{2,1,0:T(8,128)}, u32[]{:S(2)}) copy-start(f32[1,2048,512]{2,1,0:T(8,128)} %copy-done.1) | copy-start | bytes 12582916
  157.9 95.8 %copy-start.19 = (f32[1,128,512]{2,0,1:T(1,128)}, f32[1,128,512]{2,0,1:T(1,128)S(1)}, u32[]{:S(2)}) copy-start(f32[1,128,512]{2,0,1:T(1,128)S(1)} %get-tuple-element.47) | copy-start | bytes 786436
  173.7 79.9 %copy-start.20 = (f32[1,128,512]{2,0,1:T(1,128)}, f32[1,128,512]{2,0,1:T(1,128)S(1)}, u32[]{:S(2)}) copy-start(f32[1,128,512]{2,0,1:T(1,128)S(1)} %get-tuple-element.54) | copy-start | bytes 786436
  245.2 11.9 %copy-start.21 = (f32[1,128,512]{2,0,1:T(1,128)S(1)}, f32[1,128,512]{2,0,1:T(1,128)}, u32[]{:S(2)}) copy-start(f32[1,128,512]{2,0,1:T(1,128)} %get-tuple-element.44) | copy-start | bytes 786436
  245.2 11.9 %copy-start.22 = (f32[1,128,512]{2,0,1:T(1,128)S(1)}, f32[1,128,512]{2,0,1:T(1,128)}, u32[]{:S(2)}) copy-start(f32[1,128,512]{2,0,1:T(1,128)} %get-tuple-element.43) | copy-start | bytes 786436
  245.2 12.0 %copy-start.23 = (f32[1,128,512]{2,0,1:T(1,128)S(1)}, f32[1,128,512]{2,0,1:T(1,128)}, u32[]{:S(2)}) copy-start(f32[1,128,512]{2,0,1:T(1,128)} %get-tuple-element.51) | copy-start | bytes 786436
  245.2 12.0 %copy-start.24 = (f32[1,128,512]{2,0,1:T(1,128)S(1)}, f32[1,128,512]{2,0,1:T(1,128)}, u32[]{:S(2)}) copy-start(f32[1,128,512]{2,0,1:T(1,128)} %get-tuple-element.50) | copy-start | bytes 786436
  246.6 17.5 %copy-start.9 = (f32[1,2048,512]{2,1,0:T(8,128)S(1)}, f32[1,2048,512]{2,1,0:T(8,128)}, u32[]{:S(2)}) copy-start(f32[1,2048,512]{2,1,0:T(8,128)} %copy-done.8) | copy-start | bytes 12582916
  257.0 7.1 copy-start.5
  257.0 7.1 copy-start.12
  257.0 7.1 copy-start.13
  257.1 7.1 copy-start.14
  257.1 7.1 copy-start.15
  257.1 7.1 copy-start.16
  257.1 7.1 copy-start.17
  269.4 6.5 copy-start.30
  272.6 7.6 copy-start.36
  272.6 7.6 copy-start.37
  272.6 7.6 copy-start.38
  272.6 7.6 copy-start.39
  272.7 7.6 copy-start.40
  272.7 7.6 copy-start.41
  280.3 13.0 %copy-start.31 = (f32[1,1,128,512]{3,0,2,1:T(1,128)S(1)}, f32[1,1,128,512]{3,0,2,1:T(1,128)}, u32[]{:S(2)}) copy-start(f32[1,1,128,512]{3,0,2,1:T(1,128)} %get-tuple-element.70) | copy-start | bytes 786436
  280.3 13.0 %copy-start.32 = (f32[1,1,128,512]{3,0,2,1:T(1,128)S(1)}, f32[1,1,128,512]{3,0,2,1:T(1,128)}, u32[]{:S(2)}) copy-start(f32[1,1,128,512]{3,0,2,1:T(1,128)} %get-tuple-element.71) | copy-start | bytes 786436
  280.3 13.0 %copy-start.33 = (f32[1,1,128,512]{3,0,2,1:T(1,128)S(1)}, f32[1,1,128,512]{3,0,2,1:T(1,128)}, u32[]{:S(2)}) copy-start(f32[1,1,128,512]{3,0,2,1:T(1,128)} %get-tuple-element.72) | copy-start | bytes 786436
  280.3 13.0 %copy-start.34 = (f32[1,1,128,512]{3,0,2,1:T(1,128)S(1)}, f32[1,1,128,512]{3,0,2,1:T(1,128)}, u32[]{:S(2)}) copy-start(f32[1,1,128,512]{3,0,2,1:T(1,128)} %get-tuple-element.97) | copy-start | bytes 786436
  280.3 13.0 %copy-start.35 = (f32[1,1,128,512]{3,0,2,1:T(1,128)S(1)}, f32[1,1,128,512]{3,0,2,1:T(1,128)}, u32[]{:S(2)}) copy-start(f32[1,1,128,512]{3,0,2,1:T(1,128)} %get-tuple-element.98) | copy-start | bytes 786436
  293.3 13.0 %copy-start.11 = (bf16[1,2048,512]{2,1,0:T(8,128)(2,1)S(1)}, bf16[1,2048,512]{2,1,0:T(8,128)(2,1)}, u32[]{:S(2)}) copy-start(bf16[1,2048,512]{2,1,0:T(8,128)(2,1)} %param.21) | copy-start | bytes 6291460
  293.3 13.0 %copy-start.43 = (f32[1,2048]{1,0:T(1,128)S(1)}, f32[1,2048]{1,0:T(1,128)}, u32[]{:S(2)}) copy-start(f32[1,2048]{1,0:T(1,128)} %copy-done.42) | copy-start | bytes 24580
  293.3 13.0 %copy-start.49 = (f32[1,2048]{1,0:T(1,128)S(1)}, f32[1,2048]{1,0:T(1,128)}, u32[]{:S(2)}) copy-start(f32[1,2048]{1,0:T(1,128)} %copy-done.48) | copy-start | bytes 24580
  293.4 13.0 %copy-start.52 = (f32[512]{0:T(512)S(1)}, f32[512]{0:T(512)}, u32[]{:S(2)}) copy-start(f32[512]{0:T(512)} %param.18) | copy-start | bytes 6148
  293.4 13.0 %copy-start.54 = (f32[512]{0:T(512)S(1)}, f32[512]{0:T(512)}, u32[]{:S(2)}) copy-start(f32[512]{0:T(512)} %param.16) | copy-start | bytes 6148
  293.4 13.0 %copy-start.58 = (f32[512]{0:T(512)S(1)}, f32[512]{0:T(512)}, u32[]{:S(2)}) copy-start(f32[512]{0:T(512)} %param.17) | copy-start | bytes 6148
  444.3 419.3 %all-reduce.36.cloned.1.call-start = ((), (), s32[]{:S(2)}) async-start(), calls=%async_computation.3 | async-start | bytes 25165824 | tf_op jit(solution)/shard_map/psum | solution.py:152
  (20 other events, 74.2 us)
Sparse Core Ops, SparseCore 0:
  444.4 125.0 reduce-scatter.1
Sparse Core Ops, SparseCore 1:
  468.1 395.4 all-reduce.35
